TPU v7x, 256 devices: a whole 4x4x8 slice. The times are simulated.
256 devices in a mesh: dp: 32 (over x, y, core), mp: 8 (over z).
Axes of the slice: x: 4, y: 4, z: 8, core: 2. Of those that a mesh axis runs over, the one named last changes fastest.
Arguments:
- features: bfloat16 [65536, 2, 512], P('dp'), may hold values from -27 to 27
- projection: bfloat16 [512, 256], replicated, may hold values from -1 to 1
- prototypes: float32 [3000, 256], P('mp'), may hold values from -7 to 7
Outputs:
- grad_prototypes: float32 [3000, 256], P('mp')
- grad_projection: float32 [512, 256], replicated
- loss: float32 [], replicated
All inputs are finite; a program needn't handle non-finite values.
Results may differ from a plain program's by a relative error of at most 0.0019.
The roundings to bfloat16 on the way count: a program that leaves them out, or rounds other values in their place, can miss the bound.
Values may be sent and summed in bfloat16 or wider, within the bound.
A program may use at most 128 MiB of HBM per device.

v0:
```python
import jax
import jax.numpy as jnp
from jax import lax
from jax.sharding import PartitionSpec as P

ITERS = 3
EPSILON_CODES = 0.05
SOFTMAX_TEMPER = 0.1
LOSS_FACTOR = 4096.0
TINY = 1e-06


def unit_rows(values):
    inverse = lax.rsqrt(jnp.sum(values * values, axis=-1, keepdims=True) + TINY)
    return (values * inverse, inverse)


def prototype_totals(values):
    return lax.psum(jnp.sum(values, axis=0), "dp")


def code_totals(values):
    return lax.psum(jnp.sum(values, axis=-1), "mp")


def loss_pieces(
    prototype_logits, softmax_exponent, softmax_denominator, assignments, gradient_factor
):
    swapped_targets = assignments[:, ::-1]
    grad_half = (
        (softmax_exponent / softmax_denominator[..., None] - swapped_targets) * gradient_factor
    ).astype(jnp.bfloat16)
    loss_portion = jnp.sum(
        swapped_targets
        * (prototype_logits * (1.0 / SOFTMAX_TEMPER) - jnp.log(softmax_denominator)[..., None])
    )
    return (grad_half, loss_portion)


def embed_backward(grad_unit, embed_unit, embed_inverse, own_feats):
    along_unit = jnp.sum(embed_unit * grad_unit, axis=-1, keepdims=True)
    grad_raw = ((grad_unit - embed_unit * along_unit) * embed_inverse).astype(jnp.bfloat16)
    return jnp.einsum("bve,bvp->ep", own_feats, grad_raw, preferred_element_type=jnp.float32)


def body(features, projection, prototypes):
    local_rows = features.shape[0]
    own_count = local_rows // lax.axis_size("mp")
    batch_row_count = local_rows * lax.axis_size("dp")
    gradient_factor = LOSS_FACTOR / (2.0 * batch_row_count * SOFTMAX_TEMPER)
    proto_unit, proto_inverse = unit_rows(prototypes)
    proto_half = proto_unit.astype(jnp.bfloat16)
    first_row = lax.axis_index("mp") * own_count
    own_feats = lax.dynamic_slice_in_dim(features, first_row, own_count, 0)
    raw_embed = jnp.einsum("bve,ep->bvp", own_feats, projection, preferred_element_type=jnp.float32)
    embed_unit, embed_inverse = unit_rows(raw_embed)
    embed_half = embed_unit.astype(jnp.bfloat16)
    all_embed = lax.all_gather(embed_half, "mp", axis=0, tiled=True)
    prototype_logits = jnp.einsum(
        "bvp,kp->bvk", all_embed, proto_half, preferred_element_type=jnp.float32
    )
    transport = jnp.exp(prototype_logits * (1.0 / EPSILON_CODES))
    softmax_exponent = jnp.exp(prototype_logits * (1.0 / SOFTMAX_TEMPER))
    soft_part = jnp.sum(softmax_exponent, axis=-1)
    for iteration in range(ITERS - 1):
        transport = transport / prototype_totals(transport)[None]
        transport = transport / code_totals(transport)[..., None]
    transport = transport / prototype_totals(transport)[None]
    softmax_denominator = lax.psum(soft_part, "mp")
    row_sums = code_totals(transport)
    assignments = transport / row_sums[..., None]
    grad_half, loss_portion = loss_pieces(
        prototype_logits, softmax_exponent, softmax_denominator, assignments, gradient_factor
    )
    proto_grad = jnp.einsum("bvk,bvp->kp", grad_half, all_embed, preferred_element_type=jnp.float32)
    proto_grad = lax.psum(proto_grad, "dp")
    grad_unit = lax.psum_scatter(
        jnp.einsum("bvk,kp->bvp", grad_half, proto_half, preferred_element_type=jnp.float32),
        "mp",
        scatter_dimension=0,
        tiled=True,
    )
    weight_part = embed_backward(grad_unit, embed_unit, embed_inverse, own_feats)
    weight_grad, loss_total = lax.psum((weight_part, loss_portion), ("dp", "mp"))
    along_proto = jnp.sum(proto_unit * proto_grad, axis=-1, keepdims=True)
    grad_protos = (proto_grad - proto_unit * along_proto) * proto_inverse
    loss_value = -loss_total / (2.0 * batch_row_count)
    return (grad_protos, weight_grad, loss_value)


def solution(mesh):
    return jax.shard_map(
        body,
        mesh=mesh,
        in_specs=(P("dp", None, None), P(), P("mp", None)),
        out_specs=(P("mp", None), P(), P()),
        check_vma=False,
    )
```

profile of v0, /device:TPU:2, one launch (start us, length us, event | category | flops | bytes accessed | tf_op | source)
XLA Modules:
  0.0 803.6 jit_solution(7048572155357733132)
XLA Ops:
  7.2 1.4 constant_dynamic-slice_fusion
  8.7 0.8 copy-done.3
  9.5 0.4 multiply_reduce_fusion.1
  9.9 0.7 multiply_convert_fusion.1
  10.7 1.1 multiply_reduce_fusion.4
  11.8 49.1 %all-gather.2.cloned.1.call-done = bf16[2048,2,256]{0,2,1:T(8,128)(2,1)} async-done(((bf16[256,2,256]{0,2,1:T(8,128)(2,1)}), bf16[2048,2,256]{0,2,1:T(8,128)(2,1)}) %all-gather.2.cloned.1.call-update) | async-done | bytes 2097168 | tf_op jit(solution)/shard_map/all_gather | solution.py:58
  60.9 5.4 fusion.12
  66.3 53.0 %psum.71 = f32[2,375]{1,0:T(2,128)S(1)} all-reduce(f32[2,375]{1,0:T(2,128)S(1)} %get-tuple-element.11), channel_id=1, replica_groups=mesh['dp'=32,'mp'=8] {'dp'}, use_global_device_ids=true, to_apply=%region_5.0 | all-reduce | flops 750 | bytes 6000 | tf_op jit(solution)/shard_map/psum | solution.py:19
  119.3 3.8 exponential_reduce_fusion
  123.2 29.9 %psum.72 = f32[2048,2]{0,1:T(2,128)S(1)} all-reduce(f32[2048,2]{0,1:T(2,128)S(1)} %get-tuple-element.4), channel_id=1, replica_groups=mesh['dp'=32,'mp'=8] {'mp'}, use_global_device_ids=true, to_apply=%region_7.0 | all-reduce | flops 4096 | bytes 32768 | tf_op jit(solution)/shard_map/psum | solution.py:23
  153.0 4.4 fusion.8
  157.5 54.7 %psum.73 = f32[2,375]{1,0:T(2,128)S(1)} all-reduce(f32[2,375]{1,0:T(2,128)S(1)} %fusion.8), channel_id=1, replica_groups=mesh['dp'=32,'mp'=8] {'dp'}, use_global_device_ids=true, to_apply=%region_9.0 | all-reduce | flops 750 | bytes 6000 | tf_op jit(solution)/shard_map/psum | solution.py:19
  212.1 3.7 fusion.9
  215.9 27.0 %psum.74 = f32[2048,2]{0,1:T(2,128)S(1)} all-reduce(f32[2048,2]{0,1:T(2,128)S(1)} %fusion.9), channel_id=1, replica_groups=mesh['dp'=32,'mp'=8] {'mp'}, use_global_device_ids=true, to_apply=%region_11.0 | all-reduce | flops 4096 | bytes 32768 | tf_op jit(solution)/shard_map/psum | solution.py:23
  242.9 3.9 fusion.10
  246.8 62.7 %psum.75 = f32[2,375]{1,0:T(2,128)S(1)} all-reduce(f32[2,375]{1,0:T(2,128)S(1)} %fusion.10), channel_id=1, replica_groups=mesh['dp'=32,'mp'=8] {'dp'}, use_global_device_ids=true, to_apply=%region_13.0 | all-reduce | flops 750 | bytes 6000 | tf_op jit(solution)/shard_map/psum | solution.py:19
  309.5 4.3 fusion.11
  313.8 27.7 %all-reduce = (f32[2048,2]{0,1:T(2,128)S(1)}, f32[2048,2]{0,1:T(2,128)S(1)}) all-reduce(f32[2048,2]{0,1:T(2,128)S(1)} %fusion.11, f32[2048,2]{0,1:T(2,128)S(1)} %get-tuple-element.3), channel_id=1, replica_groups=mesh['dp'=32,'mp'=8] {'mp'}, use_global_device_ids=true, to_apply=%region_15.0 | all-reduce | flops 8192 | bytes 65536 | tf_op jit(solution)/shard_map/psum | solution.py:23
  341.5 5.1 fusion.7
  346.7 2.6 multiply_reduce_fusion
  349.2 1.6 copy-done.1
  350.9 3.3 fusion.28
  354.2 0.0 all-reduce.4.cloned.1.call-start
  354.3 4.3 convolution_bitcast_fusion.1
  358.7 0.0 all-reduce.6.cloned.1.call-start
  358.7 90.6 %psum.79 = f32[]{:T(128)} all-reduce(f32[]{:T(128)} %get-tuple-element.7), channel_id=1, replica_groups=mesh['dp'=32,'mp'=8] {'dp','mp'}, use_global_device_ids=true, to_apply=%region_22.0 | all-reduce | flops 1 | bytes 8 | tf_op jit(solution)/shard_map/psum | solution.py:84
  450.0 2.5 convolution_bitcast_fusion
  452.5 83.7 %all-reduce.4.cloned.1.call-done = f32[375,256]{1,0:T(8,128)} async-done(((f32[375,256]{1,0:T(8,128)}), f32[375,256]{1,0:T(8,128)}) %all-reduce.4.cloned.1.call-update) | async-done | bytes 384016 | tf_op jit(solution)/shard_map/psum | solution.py:76
  536.2 1.2 multiply_reduce_fusion.3
  537.4 1.9 subtract_multiply_fusion
  539.3 254.8 %all-reduce.6.cloned.1.call-done = f32[512,256]{1,0:T(8,128)} async-done(((f32[512,256]{1,0:T(8,128)}), f32[512,256]{1,0:T(8,128)}) %all-reduce.6.cloned.1.call-update) | async-done | bytes 524304 | tf_op jit(solution)/shard_map/psum | solution.py:84
  794.1 1.9 copy.29
  (23 shorter events, 0.2 us)
Async XLA Ops:
  7.2 2.3 copy-start
  7.2 53.7 %all-gather.2.cloned.1.call-start = ((), (), s32[]{:S(2)}) async-start(), calls=%async_computation.1 | async-start | bytes 2359296 | tf_op jit(solution)/shard_map/all_gather | solution.py:58
  8.7 0.8 copy-start.3
  10.6 439.3 %reduce-scatter.2.cloned.1.call-start = ((), (), s32[]{:S(2)}) async-start(), calls=%async_computation.3 | async-start | bytes 4718592 | tf_op jit(solution)/shard_map/reduce_scatter | solution.py:77
  309.5 37.1 %slice-start = ((s8[6160384]{0:T(1024)(128)(4,1)}), s8[1966080]{0:T(1024)(128)(4,1)S(1)}, s32[]{:S(2)}) async-start(s8[6160384]{0:T(1024)(128)(4,1)} %bitcast.19), calls=%async_computation.5 | async-start | bytes 3932160
  341.5 5.1 slice-start.1
  346.7 4.2 copy-start.2
  349.2 1.6 copy-start.1
  354.2 95.8 %copy-start.4 = (bf16[256,2,512]{2,1,0:T(2,128)(2,1)S(1)}, bf16[256,2,512]{2,1,0:T(2,128)(2,1)}, u32[]{:S(2)}) copy-start(bf16[256,2,512]{2,1,0:T(2,128)(2,1)} %copy-done.3) | copy-start | bytes 1572868
  354.2 181.9 %all-reduce.4.cloned.1.call-start = ((), (), s32[]{:S(2)}) async-start(), calls=%async_computation.2 | async-start | bytes 770048 | tf_op jit(solution)/shard_map/psum | solution.py:76
  358.7 435.4 %all-reduce.6.cloned.1.call-start = ((), (), s32[]{:S(2)}) async-start(), calls=%async_computation.4 | async-start | bytes 1048576 | tf_op jit(solution)/shard_map/psum | solution.py:84
Sparse Core Ops, SparseCore 0:
  10.7 50.1 all-gather.1
  354.4 66.9 reduce-scatter.1
  425.2 110.8 all-reduce.3
  542.1 251.9 all-reduce.5
where the time goes:
time: 804 us
  waiting for transfers between devices  388 us (48%)
  blocking collectives  345 us (43%)
  other arithmetic  32.9 us (4%)
  matrix products  16 us (2%)
  between operations  15.7 us (2%)
    psum x1, waiting for transfers between devices, body(): lax.psum((weight_part, loss_portion), ('dp', 'mp'))  255 us
    psum x3, blocking collectives, prototype_totals(): return lax.psum(jnp.sum(values, axis=0), 'dp')  170 us
    psum x1, blocking collectives, body(): lax.psum((weight_part, loss_portion), ('dp', 'mp'))  90.6 us
    psum x3, blocking collectives, code_totals(): return lax.psum(jnp.sum(values, axis=-1), 'mp')  84.6 us
    psum x1, waiting for transfers between devices, body(): proto_grad = lax.psum(proto_grad, 'dp')  83.7 us
    all_gather x1, waiting for transfers between devices, body(): all_embed = lax.all_gather(embed_half, 'mp', axis=0, tiled=True)  49.1 us
  transfers between devices with their start and end apart: 4, of which 3 were waited for; matrix products, arithmetic and copies ran while one was open for 1% of the time, Pallas kernels for 0%

commit v1 on v0

--- a/solution.py
+++ b/solution.py
@@ -8,6 +8,12 @@
 SOFTMAX_TEMPER = 0.1
 LOSS_FACTOR = 4096.0
 TINY = 1e-06
+
+
+def gather_and_add(shard, axis):
+    parts = lax.all_gather(shard, axis, axis=0, tiled=False)
+    total = parts.sum(axis=0)
+    return total
 
 
 def unit_rows(values):
@@ -73,7 +79,7 @@
         prototype_logits, softmax_exponent, softmax_denominator, assignments, gradient_factor
     )
     proto_grad = jnp.einsum("bvk,bvp->kp", grad_half, all_embed, preferred_element_type=jnp.float32)
-    proto_grad = lax.psum(proto_grad, "dp")
+    proto_grad = gather_and_add(proto_grad, "dp")
     grad_unit = lax.psum_scatter(
         jnp.einsum("bvk,kp->bvp", grad_half, proto_half, preferred_element_type=jnp.float32),
         "mp",

time: 804 us -> 758 us (0.943)
  waiting for transfers between devices: 388 us -> 338 us
    psum x1 -> x0, waiting for transfers between devices: 83.7 us -> none  [body(): proto_grad = lax.psum(proto_grad, 'dp')]
    all_gather x0 -> x1, waiting for transfers between devices: none -> 37.5 us  [gather_and_add(): parts = lax.all_gather(shard, axis, axis=0, tiled=False)]
  transfers between devices with their start and end apart: 4 -> 4, of which waited for: 3 -> 3; matrix products, arithmetic and copies ran while one was open for 1% -> 2% of each run, Pallas kernels for 0% -> 0%
where the time goes in v1:
time: 758 us; the launch traced here: 757 us
  blocking collectives  346 us (46%)
  waiting for transfers between devices  338 us (45%)
  other arithmetic  36.3 us (5%)
  matrix products  16 us (2%)
  between operations  15.7 us (2%)
    psum x1, waiting for transfers between devices, body(): lax.psum((weight_part, loss_portion), ('dp', 'mp'))  251 us
    psum x3, blocking collectives, prototype_totals(): return lax.psum(jnp.sum(values, axis=0), 'dp')  170 us
    psum x1, blocking collectives, body(): lax.psum((weight_part, loss_portion), ('dp', 'mp'))  91 us
    psum x3, blocking collectives, code_totals(): return lax.psum(jnp.sum(values, axis=-1), 'mp')  84.6 us
    all_gather x1, waiting for transfers between devices, body(): all_embed = lax.all_gather(embed_half, 'mp', axis=0, tiled=True)  49.1 us
    all_gather x1, waiting for transfers between devices, gather_and_add(): parts = lax.all_gather(shard, axis, axis=0, tiled=False)  37.5 us
  transfers between devices with their start and end apart: 4, of which 3 were waited for; matrix products, arithmetic and copies ran while one was open for 2% of the time, Pallas kernels for 0%

profile of v1, /device:TPU:2, one launch (start us, length us, event | category | flops | bytes accessed | tf_op | source)
XLA Modules:
  0.0 757.4 jit_solution(5588276538945294152)
XLA Ops:
  7.2 1.4 constant_dynamic-slice_fusion
  8.7 0.8 copy-done.3
  9.5 0.4 multiply_reduce_fusion.1
  9.9 0.7 multiply_convert_fusion.1
  10.7 1.1 multiply_reduce_fusion.4
  11.8 49.1 %all-gather.5.cloned.1.call-done = bf16[2048,2,256]{0,2,1:T(8,128)(2,1)} async-done(((bf16[256,2,256]{0,2,1:T(8,128)(2,1)}), bf16[2048,2,256]{0,2,1:T(8,128)(2,1)}) %all-gather.5.cloned.1.call-update) | async-done | bytes 2097168 | tf_op jit(solution)/shard_map/all_gather | solution.py:64
  60.9 5.4 fusion.12
  66.3 53.0 %psum.64 = f32[2,375]{1,0:T(2,128)S(1)} all-reduce(f32[2,375]{1,0:T(2,128)S(1)} %get-tuple-element.11), channel_id=1, replica_groups=mesh['dp'=32,'mp'=8] {'dp'}, use_global_device_ids=true, to_apply=%region_5.0 | all-reduce | flops 750 | bytes 6000 | tf_op jit(solution)/shard_map/psum | solution.py:25
  119.3 3.8 exponential_reduce_fusion
  123.2 29.9 %psum.65 = f32[2048,2]{0,1:T(2,128)S(1)} all-reduce(f32[2048,2]{0,1:T(2,128)S(1)} %get-tuple-element.4), channel_id=1, replica_groups=mesh['dp'=32,'mp'=8] {'mp'}, use_global_device_ids=true, to_apply=%region_7.0 | all-reduce | flops 4096 | bytes 32768 | tf_op jit(solution)/shard_map/psum | solution.py:29
  153.0 4.4 fusion.8
  157.5 54.7 %psum.66 = f32[2,375]{1,0:T(2,128)S(1)} all-reduce(f32[2,375]{1,0:T(2,128)S(1)} %fusion.8), channel_id=1, replica_groups=mesh['dp'=32,'mp'=8] {'dp'}, use_global_device_ids=true, to_apply=%region_9.0 | all-reduce | flops 750 | bytes 6000 | tf_op jit(solution)/shard_map/psum | solution.py:25
  212.1 3.7 fusion.9
  215.9 27.0 %psum.67 = f32[2048,2]{0,1:T(2,128)S(1)} all-reduce(f32[2048,2]{0,1:T(2,128)S(1)} %fusion.9), channel_id=1, replica_groups=mesh['dp'=32,'mp'=8] {'mp'}, use_global_device_ids=true, to_apply=%region_11.0 | all-reduce | flops 4096 | bytes 32768 | tf_op jit(solution)/shard_map/psum | solution.py:29
  242.9 3.9 fusion.10
  246.8 62.7 %psum.68 = f32[2,375]{1,0:T(2,128)S(1)} all-reduce(f32[2,375]{1,0:T(2,128)S(1)} %fusion.10), channel_id=1, replica_groups=mesh['dp'=32,'mp'=8] {'dp'}, use_global_device_ids=true, to_apply=%region_13.0 | all-reduce | flops 750 | bytes 6000 | tf_op jit(solution)/shard_map/psum | solution.py:25
  309.5 4.3 fusion.11
  313.8 27.7 %all-reduce = (f32[2048,2]{0,1:T(2,128)S(1)}, f32[2048,2]{0,1:T(2,128)S(1)}) all-reduce(f32[2048,2]{0,1:T(2,128)S(1)} %fusion.11, f32[2048,2]{0,1:T(2,128)S(1)} %get-tuple-element.3), channel_id=1, replica_groups=mesh['dp'=32,'mp'=8] {'mp'}, use_global_device_ids=true, to_apply=%region_15.0 | all-reduce | flops 8192 | bytes 65536 | tf_op jit(solution)/shard_map/psum | solution.py:29
  341.5 5.1 fusion.7
  346.7 2.6 multiply_reduce_fusion
  349.2 1.6 copy-done.1
  350.9 3.4 fusion.28
  354.3 0.0 all-gather.7.cloned.1.call-start
  354.3 4.3 convolution_bitcast_fusion.1
  358.7 91.0 %psum.71 = f32[]{:T(128)} all-reduce(f32[]{:T(128)} %get-tuple-element.7), channel_id=1, replica_groups=mesh['dp'=32,'mp'=8] {'dp','mp'}, use_global_device_ids=true, to_apply=%region_22.0 | all-reduce | flops 1 | bytes 8 | tf_op jit(solution)/shard_map/psum | solution.py:90
  450.4 2.5 convolution_bitcast_fusion
  452.9 37.5 %all-gather.7.cloned.1.call-done = f32[32,375,256]{2,1,0:T(8,128)} async-done(((f32[1,375,256]{2,1,0:T(8,128)}), f32[32,375,256]{2,1,0:T(8,128)}) %all-gather.7.cloned.1.call-update) | async-done | bytes 12288016 | tf_op jit(solution)/shard_map/all_gather | solution.py:14
  490.4 5.3 reduce_sum.126
  495.8 0.2 multiply_reduce_fusion.3
  496.0 0.9 subtract_multiply_fusion
  496.9 251.0 %all-reduce.3.cloned.1.call-done = f32[512,256]{1,0:T(8,128)} async-done(((f32[512,256]{1,0:T(8,128)}), f32[512,256]{1,0:T(8,128)}) %all-reduce.3.cloned.1.call-update) | async-done | bytes 524304 | tf_op jit(solution)/shard_map/psum | solution.py:90
  747.9 1.9 copy.35
  (24 shorter events, 0.3 us)
Async XLA Ops:
  7.2 2.3 copy-start
  7.2 53.7 %all-gather.5.cloned.1.call-start = ((), (), s32[]{:S(2)}) async-start(), calls=%async_computation.1 | async-start | bytes 2359296 | tf_op jit(solution)/shard_map/all_gather | solution.py:64
  8.7 0.8 copy-start.3
  10.6 439.8 %reduce-scatter.2.cloned.1.call-start = ((), (), s32[]{:S(2)}) async-start(), calls=%async_computation.2 | async-start | bytes 4718592 | tf_op jit(solution)/shard_map/reduce_scatter | solution.py:83
  309.5 37.1 %slice-start = ((s8[6160384]{0:T(1024)(128)(4,1)}), s8[1966080]{0:T(1024)(128)(4,1)S(1)}, s32[]{:S(2)}) async-start(s8[6160384]{0:T(1024)(128)(4,1)} %bitcast.20), calls=%async_computation.5 | async-start | bytes 3932160
  341.5 5.1 slice-start.1
  346.7 4.2 copy-start.2
  349.2 1.6 copy-start.1
  354.3 96.1 %copy-start.4 = (bf16[256,2,512]{2,1,0:T(2,128)(2,1)S(1)}, bf16[256,2,512]{2,1,0:T(2,128)(2,1)}, u32[]{:S(2)}) copy-start(bf16[256,2,512]{2,1,0:T(2,128)(2,1)} %copy-done.3) | copy-start | bytes 1572868
  354.3 136.2 %all-gather.7.cloned.1.call-start = ((), (), s32[]{:S(2)}) async-start(), calls=%async_computation.4 | async-start | bytes 12705792 | tf_op jit(solution)/shard_map/all_gather | solution.py:14
  358.7 389.2 %all-reduce.3.cloned.1.call-start = ((), (), s32[]{:S(2)}) async-start(), calls=%async_computation.3 | async-start | bytes 1048576 | tf_op jit(solution)/shard_map/psum | solution.py:90
Sparse Core Ops, SparseCore 0:
  10.7 50.1 all-gather.4
  354.4 66.9 reduce-scatter.1
  424.6 65.8 all-gather.6
  496.3 251.5 all-reduce.2
